TPU v7x, 1024 devices: a whole 4x8x16 slice. The times are simulated.
1024 devices in a mesh: slow: 32 (over y, x_hi, core), fast: 32 (over x_lo, z).
Axes of the slice: x: 4 (x_hi: 2, x_lo: 2; x = x_hi * 2 + x_lo), y: 8, z: 16, core: 2. Of those that a mesh axis runs over, the one named last changes fastest.
Arguments:
- query_act: bfloat16 [131072, 512], P(('slow', 'fast')), may hold values from -6 to 6
- key_act: bfloat16 [131072, 512], P(('slow', 'fast')), may hold values from -6 to 6
- value_act: bfloat16 [131072, 512], P(('slow', 'fast')), may hold values from -6 to 6
- long_filter: bfloat16 [131072, 32], P(('slow', 'fast')), may hold values from -4 to 4
- out_grad: bfloat16 [131072, 512], P(('slow', 'fast')), may hold values from -6 to 6
Outputs:
- mixed_out: bfloat16 [131072, 512], P(('slow', 'fast'))
- query_grad: bfloat16 [131072, 512], P(('slow', 'fast'))
- key_grad: bfloat16 [131072, 512], P(('slow', 'fast'))
- value_grad: bfloat16 [131072, 512], P(('slow', 'fast'))
- filter_grad: float32 [131072, 32], P(('slow', 'fast'))
All inputs are finite; a program needn't handle non-finite values.
Results may differ from a plain program's by a relative error of at most 0.0049.
Values may be sent and summed in bfloat16 or wider, within the bound.
A program may use at most 32 MiB of HBM per device.

v0:
```python
import math

import jax
import jax.numpy as jnp
from jax import lax
from jax.sharding import PartitionSpec as P

highest = lax.Precision.HIGHEST


def index_ramp(points, along, ndim, offset):
    shape_list = [1] * ndim
    shape_list[along] = points
    return (jnp.arange(points, dtype=jnp.int32) + offset).reshape(shape_list)


def apply_dft(re_im, points, direction, along):
    index_row = jnp.arange(points, dtype=jnp.int32)
    phase_turns = index_row[:, None] * index_row[None, :] % points
    phases = 2.0 * math.pi / points * phase_turns.astype(jnp.float32)
    cosine = jnp.cos(phases)
    sine_part = direction * jnp.sin(phases)

    def contract(values, matrix):
        result = jnp.tensordot(values, matrix, axes=((along,), (1,)), precision=highest)
        return jnp.moveaxis(result, -1, along)

    return (
        contract(re_im[0], cosine) - contract(re_im[1], sine_part),
        contract(re_im[0], sine_part) + contract(re_im[1], cosine),
    )


def rotate(re_im, phase_turns, period, direction):
    phases = 2.0 * math.pi / period * (phase_turns % period).astype(jnp.float32)
    cosine = jnp.cos(phases)
    sine_part = direction * jnp.sin(phases)
    return (re_im[0] * cosine - re_im[1] * sine_part, re_im[0] * sine_part + re_im[1] * cosine)


def complex_times(left, right):
    return (left[0] * right[0] - left[1] * right[1], left[0] * right[1] + left[1] * right[0])


def conj_times(left, right):
    return (left[0] * right[0] + left[1] * right[1], left[0] * right[1] - left[1] * right[0])


def positions(grid_info, slow_points, slow_offset, fast_points, fast_offset):
    fast_count, tokens = (grid_info[1], grid_info[2])
    block_index = index_ramp(slow_points, 2, 5, slow_offset) * fast_count + index_ramp(
        fast_points, 3, 5, fast_offset
    )
    return block_index * tokens + index_ramp(tokens, 4, 5, 0)


def open_halves(re_im, grid_info, fast_offset):
    token_place = positions(grid_info, re_im[0].shape[1], 0, re_im[0].shape[2], fast_offset)
    return rotate(
        (re_im[0][None], re_im[1][None]),
        index_ramp(2, 0, 5, 0) * token_place,
        2 * grid_info[3],
        -1.0,
    )


def fold_halves(re_im, token_place, seq_length):
    turned = rotate(re_im, index_ramp(2, 0, 5, 0) * token_place, 2 * seq_length, 1.0)
    scale = 0.5 / seq_length
    return (jnp.sum(turned[0], axis=0) * scale, jnp.sum(turned[1], axis=0) * scale)


def front_forward(re_im, grid_info, fast_offset):
    slow_count, fast_count = (grid_info[0], grid_info[1])
    re_im = apply_dft(re_im, slow_count, -1.0, 2)
    phase_turns = index_ramp(slow_count, 2, 5, 0) * index_ramp(re_im[0].shape[3], 3, 5, fast_offset)
    return rotate(re_im, phase_turns, slow_count * fast_count, -1.0)


def front_inverse(re_im, grid_info, fast_offset):
    slow_count, fast_count = (grid_info[0], grid_info[1])
    phase_turns = index_ramp(slow_count, 2, 5, 0) * index_ramp(re_im[0].shape[3], 3, 5, fast_offset)
    re_im = rotate(re_im, phase_turns, slow_count * fast_count, 1.0)
    return apply_dft(re_im, slow_count, 1.0, 2)


def lead_phase(re_im, grid_info, ka_offset):
    slow_count, fast_count, tokens = (grid_info[0], grid_info[1], grid_info[2])
    lead_index = index_ramp(re_im[0].shape[2], 2, 5, ka_offset) + slow_count * index_ramp(
        fast_count, 3, 5, 0
    )
    return lead_index * index_ramp(tokens, 4, 5, 0)


def back_forward(re_im, grid_info, ka_offset):
    re_im = apply_dft(re_im, grid_info[1], -1.0, 3)
    re_im = rotate(re_im, lead_phase(re_im, grid_info, ka_offset), grid_info[3], -1.0)
    return apply_dft(re_im, grid_info[2], -1.0, 4)


def back_inverse(re_im, grid_info, ka_offset):
    re_im = apply_dft(re_im, grid_info[2], 1.0, 4)
    re_im = rotate(re_im, lead_phase(re_im, grid_info, ka_offset), grid_info[3], 1.0)
    return apply_dft(re_im, grid_info[1], 1.0, 3)


def to_channels(seq_rows):
    return lax.all_to_all(
        seq_rows.reshape(1, seq_rows.shape[0], seq_rows.shape[1]),
        "slow",
        split_axis=2,
        concat_axis=0,
        tiled=True,
    )


def merge_blocks(arrays, block_count):
    tokens = arrays[0].shape[0]
    pieces = [item.reshape(tokens, block_count, item.shape[1] // block_count) for item in arrays]
    return jnp.concatenate(pieces, axis=2).reshape(tokens, -1)


def split_columns(rows_major, widths):
    tokens, block_count = (rows_major.shape[0], rows_major.shape[1])
    result = []
    offset = 0
    for length in widths:
        result.append(
            rows_major[:, :, offset : offset + length].reshape(tokens, block_count * length)
        )
        offset += length
    return result


def real_blocks(real_part, imag_part, segments):
    pieces = []
    offset = 0
    for output_kind, length in segments:
        real_seg = real_part[:, offset : offset + length]
        imag_seg = imag_part[:, offset : offset + length]
        offset += length
        if output_kind == "pairs":
            stacked = jnp.transpose(jnp.stack((real_seg, imag_seg), axis=-1), (0, 2, 1, 3))
            pieces.append(stacked.reshape(stacked.shape[0], stacked.shape[1], 2 * length))
        else:
            pieces.append(jnp.transpose(real_seg, (0, 2, 1)))
    return jnp.concatenate(pieces, axis=2)


def segment_widths(segments):
    return [2 * length if output_kind == "pairs" else length for output_kind, length in segments]


def spread_forward(seq_rows, grid_info, fast_rank, segments):
    slow_count, fast_count = (grid_info[0], grid_info[1])
    blocks = to_channels(seq_rows).astype(jnp.float32)
    real_list = []
    imag_list = []
    offset = 0
    for length, packed in segments:
        segment = blocks[:, :, offset : offset + length]
        offset += length
        if packed:
            halves = segment.reshape(segment.shape[0], segment.shape[1], length // 2, 2)
            real_seg, imag_seg = (halves[..., 0], halves[..., 1])
        else:
            real_seg, imag_seg = (segment, jnp.zeros_like(segment))
        real_list.append(jnp.transpose(real_seg, (2, 0, 1)))
        imag_list.append(jnp.transpose(imag_seg, (2, 0, 1)))
    re_im = (
        jnp.concatenate(real_list, 0)[:, :, None, :],
        jnp.concatenate(imag_list, 0)[:, :, None, :],
    )
    re_im = front_forward(open_halves(re_im, grid_info, fast_rank), grid_info, fast_rank)
    re_im = (
        lax.all_to_all(re_im[0], "fast", split_axis=2, concat_axis=3, tiled=True),
        lax.all_to_all(re_im[1], "fast", split_axis=2, concat_axis=3, tiled=True),
    )
    return back_forward(re_im, grid_info, fast_rank * (slow_count // fast_count))


def spread_inverse(re_im, grid_info, fast_rank, slow_rank, segments):
    slow_count, fast_count, tokens, seq_length = grid_info
    re_im = back_inverse(re_im, grid_info, fast_rank * (slow_count // fast_count))
    re_im = (
        lax.all_to_all(re_im[0], "fast", split_axis=3, concat_axis=2, tiled=True),
        lax.all_to_all(re_im[1], "fast", split_axis=3, concat_axis=2, tiled=True),
    )
    re_im = front_inverse(re_im, grid_info, fast_rank)
    re_im = (
        lax.all_to_all(re_im[0], "slow", split_axis=2, concat_axis=1, tiled=True),
        lax.all_to_all(re_im[1], "slow", split_axis=2, concat_axis=1, tiled=True),
    )
    real_part, imag_part = fold_halves(
        re_im, positions(grid_info, 1, slow_rank, 1, fast_rank), seq_length
    )
    length = real_part.shape[0] // slow_count
    blocks = real_blocks(
        real_part.reshape(slow_count, length, tokens),
        imag_part.reshape(slow_count, length, tokens),
        segments,
    )
    rows_major = jnp.transpose(blocks, (1, 0, 2))
    return split_columns(rows_major, segment_widths(segments))


def regroup(re_im, length, local_groups):

    def by_group(values):
        values = values[:, :length]
        return values.reshape(
            (values.shape[0], local_groups, length // local_groups) + values.shape[2:]
        )

    return (by_group(re_im[0]), by_group(re_im[1]))


def flatten_pairs(re_im):

    def merged(values):
        return values.reshape(
            (values.shape[0], values.shape[1] * values.shape[2]) + values.shape[3:]
        )

    return (merged(re_im[0]), merged(re_im[1]))


def on_device(query_act, key_act, value_act, long_filter, out_grad):
    tokens, channels = query_act.shape
    groups = long_filter.shape[1]
    slow_count = lax.axis_size("slow")
    fast_count = lax.axis_size("fast")
    seq_length = tokens * slow_count * fast_count
    grid_info = (slow_count, fast_count, tokens, seq_length)
    group_width = channels // groups
    product = (key_act.astype(jnp.float32) * value_act.astype(jnp.float32)).astype(jnp.bfloat16)
    grad_in = (out_grad.astype(jnp.float32) * query_act.astype(jnp.float32)).astype(jnp.bfloat16)
    fast_rank = lax.axis_index("fast")
    slow_rank = lax.axis_index("slow")
    data_pairs = channels // (2 * slow_count)
    local_groups = groups // slow_count
    block_width = channels // slow_count
    spectra = spread_forward(
        merge_blocks((product, long_filter), slow_count),
        grid_info,
        fast_rank,
        ((block_width, True), (local_groups, False)),
    )
    prod_spec = regroup(spectra, data_pairs, local_groups)
    filter_spec = (spectra[0][:, data_pairs:, None], spectra[1][:, data_pairs:, None])
    convolved = spread_inverse(
        flatten_pairs(complex_times(prod_spec, filter_spec)),
        grid_info,
        fast_rank,
        slow_rank,
        (("pairs", data_pairs),),
    )[0]
    grad_spec = regroup(
        spread_forward(grad_in, grid_info, fast_rank, ((block_width, True),)),
        data_pairs,
        local_groups,
    )
    back_spec = flatten_pairs(conj_times(filter_spec, grad_spec))
    corr_spec = conj_times(prod_spec, grad_spec)
    joined = (
        jnp.concatenate((back_spec[0], jnp.sum(corr_spec[0], axis=2)), axis=1),
        jnp.concatenate((back_spec[1], jnp.sum(corr_spec[1], axis=2)), axis=1),
    )
    backward, filter_sum = spread_inverse(
        joined, grid_info, fast_rank, slow_rank, (("pairs", data_pairs), ("real", local_groups))
    )
    scale = 1.0 / math.sqrt(seq_length * group_width)
    mixed_out = (query_act.astype(jnp.float32) * convolved).astype(jnp.bfloat16)
    query_grad = (out_grad.astype(jnp.float32) * convolved).astype(jnp.bfloat16)
    key_grad = (backward * value_act.astype(jnp.float32)).astype(jnp.bfloat16)
    value_grad = (backward * key_act.astype(jnp.float32)).astype(jnp.bfloat16)
    return (mixed_out, query_grad, key_grad, value_grad, filter_sum * scale)


def solution(mesh):
    placed = (
        P(("slow", "fast"), None),
        P(("slow", "fast"), None),
        P(("slow", "fast"), None),
        P(("slow", "fast"), None),
        P(("slow", "fast"), None),
    )
    return jax.shard_map(
        on_device,
        mesh=mesh,
        in_specs=placed,
        out_specs=(
            P(("slow", "fast"), None),
            P(("slow", "fast"), None),
            P(("slow", "fast"), None),
            P(("slow", "fast"), None),
            P(("slow", "fast"), None),
        ),
        check_vma=False,
    )
```

profile of v0, /device:TPU:1, one launch (start us, length us, event | category | flops | bytes accessed | tf_op | source)
XLA Modules:
  0.0 366.7 jit_solution(3255507309012606752)
XLA Ops:
  5.5 17.7 %all-to-all-start = ((bf16[32,2,1088]{2,1,0:T(2,128)(2,1)}), bf16[32,2,1088]{2,1,0:T(2,128)(2,1)S(1)}, u32[]{:S(2)}, u32[]{:S(2)}) async-start(bf16[32,2,1088]{2,1,0:T(2,128)(2,1)} %reshape.821), calls=%async_computation | async-start | bytes 294912 | tf_op jit(solution)/shard_map/all_to_all | solution.py:108
  23.4 10.9 %all-to-all-done = bf16[32,2,1088]{2,1,0:T(2,128)(2,1)S(1)} async-done(((bf16[32,2,1088]{2,1,0:T(2,128)(2,1)}), bf16[32,2,1088]{2,1,0:T(2,128)(2,1)S(1)}, u32[]{:S(2)}, u32[]{:S(2)}) %all-to-all-start) | async-done | bytes 139296 | tf_op jit(solution)/shard_map/all_to_all | solution.py:108
  37.9 12.4 %all-to-all-start.1 = ((f32[2,9,32,1,128]{4,0,3,1,2:T(2,128)}), f32[2,9,32,1,128]{4,0,3,1,2:T(2,128)S(1)}, u32[]{:S(2)}, u32[]{:S(2)}) async-start(f32[2,9,32,1,128]{4,0,3,1,2:T(2,128)} %copy.147), calls=%async_computation.1 | async-start | bytes 589824 | tf_op jit(solution)/shard_map/all_to_all | solution.py:176
  51.2 21.1 %all-to-all-done.1 = f32[2,9,32,1,128]{4,0,3,1,2:T(2,128)S(1)} async-done(((f32[2,9,32,1,128]{4,0,3,1,2:T(2,128)}), f32[2,9,32,1,128]{4,0,3,1,2:T(2,128)S(1)}, u32[]{:S(2)}, u32[]{:S(2)}) %all-to-all-start.1) | async-done | bytes 294944 | tf_op jit(solution)/shard_map/all_to_all | solution.py:176
  72.3 4.7 %all-to-all-start.2 = ((f32[2,9,32,1,128]{4,0,3,1,2:T(2,128)}), f32[2,9,32,1,128]{4,0,3,1,2:T(2,128)S(1)}, u32[]{:S(2)}, u32[]{:S(2)}) async-start(f32[2,9,32,1,128]{4,0,3,1,2:T(2,128)} %copy.149), calls=%async_computation.2 | async-start | bytes 589824 | tf_op jit(solution)/shard_map/all_to_all | solution.py:177
  78.1 19.1 %all-to-all-done.2 = f32[2,9,32,1,128]{4,0,3,1,2:T(2,128)S(1)} async-done(((f32[2,9,32,1,128]{4,0,3,1,2:T(2,128)}), f32[2,9,32,1,128]{4,0,3,1,2:T(2,128)S(1)}, u32[]{:S(2)}, u32[]{:S(2)}) %all-to-all-start.2) | async-done | bytes 294944 | tf_op jit(solution)/shard_map/all_to_all | solution.py:177
  105.1 5.9 %all-to-all-start.4 = ((f32[2,8,1,32,128]{4,1,0,2,3:T(8,128)}), f32[2,8,1,32,128]{4,1,0,2,3:T(8,128)S(1)}, u32[]{:S(2)}, u32[]{:S(2)}) async-start(f32[2,8,1,32,128]{4,1,0,2,3:T(8,128)} %copy.152), calls=%async_computation.4 | async-start | bytes 524288 | tf_op jit(solution)/shard_map/all_to_all | solution.py:187
  112.8 16.3 %all-to-all-done.4 = f32[2,8,1,32,128]{4,1,0,2,3:T(8,128)S(1)} async-done(((f32[2,8,1,32,128]{4,1,0,2,3:T(8,128)}), f32[2,8,1,32,128]{4,1,0,2,3:T(8,128)S(1)}, u32[]{:S(2)}, u32[]{:S(2)}) %all-to-all-start.4) | async-done | bytes 262176 | tf_op jit(solution)/shard_map/all_to_all | solution.py:187
  129.1 5.6 %all-to-all-start.3 = ((f32[2,8,1,32,128]{4,1,0,2,3:T(8,128)}), f32[2,8,1,32,128]{4,1,0,2,3:T(8,128)S(1)}, u32[]{:S(2)}, u32[]{:S(2)}) async-start(f32[2,8,1,32,128]{4,1,0,2,3:T(8,128)} %copy.151), calls=%async_computation.3 | async-start | bytes 524288 | tf_op jit(solution)/shard_map/all_to_all | solution.py:186
  134.7 17.3 %all-to-all-done.3 = f32[2,8,1,32,128]{4,1,0,2,3:T(8,128)S(1)} async-done(((f32[2,8,1,32,128]{4,1,0,2,3:T(8,128)}), f32[2,8,1,32,128]{4,1,0,2,3:T(8,128)S(1)}, u32[]{:S(2)}, u32[]{:S(2)}) %all-to-all-start.3) | async-done | bytes 262176 | tf_op jit(solution)/shard_map/all_to_all | solution.py:186
  154.0 10.6 %all-to-all-start.6 = ((f32[2,8,32,1,128]{4,1,0,3,2:T(8,128)}), f32[2,8,32,1,128]{4,1,0,3,2:T(8,128)S(1)}, u32[]{:S(2)}, u32[]{:S(2)}) async-start(f32[2,8,32,1,128]{4,1,0,3,2:T(8,128)} %copy.158), calls=%async_computation.6 | async-start | bytes 524288 | tf_op jit(solution)/shard_map/all_to_all | solution.py:192
  166.4 11.0 %all-to-all-done.6 = f32[2,8,32,1,128]{4,1,0,3,2:T(8,128)S(1)} async-done(((f32[2,8,32,1,128]{4,1,0,3,2:T(8,128)}), f32[2,8,32,1,128]{4,1,0,3,2:T(8,128)S(1)}, u32[]{:S(2)}, u32[]{:S(2)}) %all-to-all-start.6) | async-done | bytes 262176 | tf_op jit(solution)/shard_map/all_to_all | solution.py:192
  182.7 11.8 %all-to-all-done.5 = f32[2,8,32,1,128]{4,1,0,3,2:T(8,128)S(1)} async-done(((f32[2,8,32,1,128]{4,1,0,3,2:T(8,128)}), f32[2,8,32,1,128]{4,1,0,3,2:T(8,128)S(1)}, u32[]{:S(2)}, u32[]{:S(2)}) %all-to-all-start.5) | async-done | bytes 262176 | tf_op jit(solution)/shard_map/all_to_all | solution.py:191
  196.6 14.7 %all_to_all.150 = bf16[32,2,1024]{2,1,0:T(2,128)(2,1)S(1)} all-to-all(bf16[32,2,1024]{2,1,0:T(2,128)(2,1)S(1)} %reshape.823), channel_id=1, replica_groups=mesh['slow'=32,'fast'=32] {'slow'}, dimensions={0} | all-to-all | bytes 262144 | tf_op jit(solution)/shard_map/all_to_all | solution.py:108
  219.2 20.0 %all-to-all-done.8 = f32[2,8,32,1,128]{4,1,0,3,2:T(8,128)S(1)} async-done(((f32[2,8,32,1,128]{4,1,0,3,2:T(8,128)}), f32[2,8,32,1,128]{4,1,0,3,2:T(8,128)S(1)}, u32[]{:S(2)}, u32[]{:S(2)}) %all-to-all-start.8) | async-done | bytes 262176 | tf_op jit(solution)/shard_map/all_to_all | solution.py:176
  239.2 4.7 %all-to-all-start.9 = ((f32[2,8,32,1,128]{4,1,0,3,2:T(8,128)}), f32[2,8,32,1,128]{4,1,0,3,2:T(8,128)S(1)}, u32[]{:S(2)}, u32[]{:S(2)}) async-start(f32[2,8,32,1,128]{4,1,0,3,2:T(8,128)} %copy.171), calls=%async_computation.9 | async-start | bytes 524288 | tf_op jit(solution)/shard_map/all_to_all | solution.py:177
  244.8 17.7 %all-to-all-done.9 = f32[2,8,32,1,128]{4,1,0,3,2:T(8,128)S(1)} async-done(((f32[2,8,32,1,128]{4,1,0,3,2:T(8,128)}), f32[2,8,32,1,128]{4,1,0,3,2:T(8,128)S(1)}, u32[]{:S(2)}, u32[]{:S(2)}) %all-to-all-start.9) | async-done | bytes 262176 | tf_op jit(solution)/shard_map/all_to_all | solution.py:177
  270.6 5.9 %all-to-all-start.11 = ((f32[2,9,1,32,128]{4,0,2,1,3:T(2,128)}), f32[2,9,1,32,128]{4,0,2,1,3:T(2,128)S(1)}, u32[]{:S(2)}, u32[]{:S(2)}) async-start(f32[2,9,1,32,128]{4,0,2,1,3:T(2,128)} %copy.175), calls=%async_computation.11 | async-start | bytes 589824 | tf_op jit(solution)/shard_map/all_to_all | solution.py:187
  277.8 17.8 %all-to-all-done.11 = f32[2,9,1,32,128]{4,0,2,1,3:T(2,128)S(1)} async-done(((f32[2,9,1,32,128]{4,0,2,1,3:T(2,128)}), f32[2,9,1,32,128]{4,0,2,1,3:T(2,128)S(1)}, u32[]{:S(2)}, u32[]{:S(2)}) %all-to-all-start.11) | async-done | bytes 294944 | tf_op jit(solution)/shard_map/all_to_all | solution.py:187
  295.6 24.3 %all_to_all.151 = f32[2,9,1,32,128]{4,0,2,1,3:T(2,128)S(1)} all-to-all(f32[2,9,1,32,128]{4,0,2,1,3:T(2,128)S(1)} %copy.173), channel_id=1, replica_groups=mesh['slow'=32,'fast'=32] {'fast'}, dimensions={3} | all-to-all | bytes 589824 | tf_op jit(solution)/shard_map/all_to_all | solution.py:186
  321.8 9.9 %all-to-all-start.13 = ((f32[2,9,32,1,128]{4,0,3,1,2:T(2,128)}), f32[2,9,32,1,128]{4,0,3,1,2:T(2,128)S(1)}, u32[]{:S(2)}, u32[]{:S(2)}) async-start(f32[2,9,32,1,128]{4,0,3,1,2:T(2,128)} %copy.178), calls=%async_computation.13 | async-start | bytes 589824 | tf_op jit(solution)/shard_map/all_to_all | solution.py:192
  333.7 11.4 %all-to-all-done.13 = f32[2,9,32,1,128]{4,0,3,1,2:T(2,128)S(1)} async-done(((f32[2,9,32,1,128]{4,0,3,1,2:T(2,128)}), f32[2,9,32,1,128]{4,0,3,1,2:T(2,128)S(1)}, u32[]{:S(2)}, u32[]{:S(2)}) %all-to-all-start.13) | async-done | bytes 294944 | tf_op jit(solution)/shard_map/all_to_all | solution.py:192
  345.1 4.5 %all-to-all-start.12 = ((f32[2,9,32,1,128]{4,0,3,1,2:T(2,128)}), f32[2,9,32,1,128]{4,0,3,1,2:T(2,128)S(1)}, u32[]{:S(2)}, u32[]{:S(2)}) async-start(f32[2,9,32,1,128]{4,0,3,1,2:T(2,128)} %copy.177), calls=%async_computation.12 | async-start | bytes 589824 | tf_op jit(solution)/shard_map/all_to_all | solution.py:191
  351.1 11.9 %all-to-all-done.12 = f32[2,9,32,1,128]{4,0,3,1,2:T(2,128)S(1)} async-done(((f32[2,9,32,1,128]{4,0,3,1,2:T(2,128)}), f32[2,9,32,1,128]{4,0,3,1,2:T(2,128)S(1)}, u32[]{:S(2)}, u32[]{:S(2)}) %all-to-all-start.12) | async-done | bytes 294944 | tf_op jit(solution)/shard_map/all_to_all | solution.py:191
  (131 shorter events, 57.9 us)
Async XLA Ops:
  1.3 1.1 copy-start
  5.5 28.8 %all-to-all-start = ((bf16[32,2,1088]{2,1,0:T(2,128)(2,1)}), bf16[32,2,1088]{2,1,0:T(2,128)(2,1)S(1)}, u32[]{:S(2)}, u32[]{:S(2)}) async-start(bf16[32,2,1088]{2,1,0:T(2,128)(2,1)} %reshape.821), calls=%async_computation | async-start | bytes 294912 | tf_op jit(solution)/shard_map/all_to_all | solution.py:108
  37.9 34.4 %all-to-all-start.1 = ((f32[2,9,32,1,128]{4,0,3,1,2:T(2,128)}), f32[2,9,32,1,128]{4,0,3,1,2:T(2,128)S(1)}, u32[]{:S(2)}, u32[]{:S(2)}) async-start(f32[2,9,32,1,128]{4,0,3,1,2:T(2,128)} %copy.147), calls=%async_computation.1 | async-start | bytes 589824 | tf_op jit(solution)/shard_map/all_to_all | solution.py:176
  72.3 24.9 %all-to-all-start.2 = ((f32[2,9,32,1,128]{4,0,3,1,2:T(2,128)}), f32[2,9,32,1,128]{4,0,3,1,2:T(2,128)S(1)}, u32[]{:S(2)}, u32[]{:S(2)}) async-start(f32[2,9,32,1,128]{4,0,3,1,2:T(2,128)} %copy.149), calls=%async_computation.2 | async-start | bytes 589824 | tf_op jit(solution)/shard_map/all_to_all | solution.py:177
  105.1 24.0 %all-to-all-start.4 = ((f32[2,8,1,32,128]{4,1,0,2,3:T(8,128)}), f32[2,8,1,32,128]{4,1,0,2,3:T(8,128)S(1)}, u32[]{:S(2)}, u32[]{:S(2)}) async-start(f32[2,8,1,32,128]{4,1,0,2,3:T(8,128)} %copy.152), calls=%async_computation.4 | async-start | bytes 524288 | tf_op jit(solution)/shard_map/all_to_all | solution.py:187
  129.1 23.0 %all-to-all-start.3 = ((f32[2,8,1,32,128]{4,1,0,2,3:T(8,128)}), f32[2,8,1,32,128]{4,1,0,2,3:T(8,128)S(1)}, u32[]{:S(2)}, u32[]{:S(2)}) async-start(f32[2,8,1,32,128]{4,1,0,2,3:T(8,128)} %copy.151), calls=%async_computation.3 | async-start | bytes 524288 | tf_op jit(solution)/shard_map/all_to_all | solution.py:186
  154.0 23.4 %all-to-all-start.6 = ((f32[2,8,32,1,128]{4,1,0,3,2:T(8,128)}), f32[2,8,32,1,128]{4,1,0,3,2:T(8,128)S(1)}, u32[]{:S(2)}, u32[]{:S(2)}) async-start(f32[2,8,32,1,128]{4,1,0,3,2:T(8,128)} %copy.158), calls=%async_computation.6 | async-start | bytes 524288 | tf_op jit(solution)/shard_map/all_to_all | solution.py:192
  166.4 15.2 %copy-start.1 = (bf16[128,512]{1,0:T(8,128)(2,1)S(1)}, bf16[128,512]{1,0:T(8,128)(2,1)}, u32[]{:S(2)}) copy-start(bf16[128,512]{1,0:T(8,128)(2,1)} %param.9) | copy-start | bytes 393220
  177.4 17.1 %all-to-all-start.5 = ((f32[2,8,32,1,128]{4,1,0,3,2:T(8,128)}), f32[2,8,32,1,128]{4,1,0,3,2:T(8,128)S(1)}, u32[]{:S(2)}, u32[]{:S(2)}) async-start(f32[2,8,32,1,128]{4,1,0,3,2:T(8,128)} %copy.155), calls=%async_computation.5 | async-start | bytes 524288 | tf_op jit(solution)/shard_map/all_to_all | solution.py:191
  181.6 0.9 copy-start.2
  214.4 24.7 %all-to-all-start.8 = ((f32[2,8,32,1,128]{4,1,0,3,2:T(8,128)}), f32[2,8,32,1,128]{4,1,0,3,2:T(8,128)S(1)}, u32[]{:S(2)}, u32[]{:S(2)}) async-start(f32[2,8,32,1,128]{4,1,0,3,2:T(8,128)} %copy.169), calls=%async_computation.8 | async-start | bytes 524288 | tf_op jit(solution)/shard_map/all_to_all | solution.py:176
  239.2 23.3 %all-to-all-start.9 = ((f32[2,8,32,1,128]{4,1,0,3,2:T(8,128)}), f32[2,8,32,1,128]{4,1,0,3,2:T(8,128)S(1)}, u32[]{:S(2)}, u32[]{:S(2)}) async-start(f32[2,8,32,1,128]{4,1,0,3,2:T(8,128)} %copy.171), calls=%async_computation.9 | async-start | bytes 524288 | tf_op jit(solution)/shard_map/all_to_all | solution.py:177
  270.6 25.0 %all-to-all-start.11 = ((f32[2,9,1,32,128]{4,0,2,1,3:T(2,128)}), f32[2,9,1,32,128]{4,0,2,1,3:T(2,128)S(1)}, u32[]{:S(2)}, u32[]{:S(2)}) async-start(f32[2,9,1,32,128]{4,0,2,1,3:T(2,128)} %copy.175), calls=%async_computation.11 | async-start | bytes 589824 | tf_op jit(solution)/shard_map/all_to_all | solution.py:187
  321.8 23.3 %all-to-all-start.13 = ((f32[2,9,32,1,128]{4,0,3,1,2:T(2,128)}), f32[2,9,32,1,128]{4,0,3,1,2:T(2,128)S(1)}, u32[]{:S(2)}, u32[]{:S(2)}) async-start(f32[2,9,32,1,128]{4,0,3,1,2:T(2,128)} %copy.178), calls=%async_computation.13 | async-start | bytes 589824 | tf_op jit(solution)/shard_map/all_to_all | solution.py:192
  345.1 17.9 %all-to-all-start.12 = ((f32[2,9,32,1,128]{4,0,3,1,2:T(2,128)}), f32[2,9,32,1,128]{4,0,3,1,2:T(2,128)S(1)}, u32[]{:S(2)}, u32[]{:S(2)}) async-start(f32[2,9,32,1,128]{4,0,3,1,2:T(2,128)} %copy.177), calls=%async_computation.12 | async-start | bytes 589824 | tf_op jit(solution)/shard_map/all_to_all | solution.py:191
where the time goes:
time: 373 us; the launch traced here: 367 us
  waiting for transfers between devices  186 us (50%)
  starting transfers between devices  89.9 us (24%)
  blocking collectives  39 us (10%)
  matrix products  25.5 us (7%)
  local copies, waits for them, and re-layouts  18.5 us (5%)
  other arithmetic  5.82 us (2%)
    all_to_all x2, waiting for transfers between devices, spread_forward(): lax.all_to_all(re_im[0], 'fast', split_axis=2, concat_axis=3, tiled=True)  41.1 us
    all_to_all x2, waiting for transfers between devices, spread_forward(): lax.all_to_all(re_im[1], 'fast', split_axis=2, concat_axis=3, tiled=True)  36.8 us
    all_to_all x2, waiting for transfers between devices, spread_inverse(): lax.all_to_all(re_im[1], 'fast', split_axis=3, concat_axis=2, tiled=True)  34.1 us
    dot_general x48, matrix products, contract(): jnp.tensordot(values, matrix, axes=((along,), (1,)), precision=highest)  25.5 us
    all_to_all x1, blocking collectives, spread_inverse(): lax.all_to_all(re_im[0], 'fast', split_axis=3, concat_axis=2, tiled=True)  24.3 us
    all_to_all x2, waiting for transfers between devices, spread_inverse(): lax.all_to_all(re_im[0], 'slow', split_axis=2, concat_axis=1, tiled=True)  23.7 us
    all_to_all x2, waiting for transfers between devices, spread_inverse(): lax.all_to_all(re_im[1], 'slow', split_axis=2, concat_axis=1, tiled=True)  22.4 us
    all_to_all x2, starting transfers between devices, spread_inverse(): lax.all_to_all(re_im[1], 'slow', split_axis=2, concat_axis=1, tiled=True)  20.6 us
  transfers between devices with their start and end apart: 12, of which 12 were waited for; matrix products, arithmetic and copies ran while one was open for 3% of the time, Pallas kernels for 0%

commit v1 on v0

v1 whole, which is shorter than its diff:
```python
import functools
import math

import jax
import jax.numpy as jnp
from jax import lax
from jax.experimental import pallas as pl
from jax.experimental.pallas import tpu as pltpu
from jax.sharding import PartitionSpec as P

MESH = pl.DeviceIdType.MESH
f32 = jnp.float32
bf16 = jnp.bfloat16
LANES = 128
BLOCK = 4


def times_const(value, factor):
    re, im = value
    a, b = factor.real, factor.imag
    if abs(b) < 1e-12:
        if abs(a - 1.0) < 1e-12:
            return re, im
        return re * a, im * a
    if abs(a) < 1e-12:
        return (-im, re) if b > 0 else (im, -re)
    return re * a - im * b, re * b + im * a


def unit(turns):
    return complex(math.cos(2.0 * math.pi * turns), math.sin(2.0 * math.pi * turns))


def dft(values, sign):
    count = len(values)
    if count == 1:
        return values
    even, odd = dft(values[0::2], sign), dft(values[1::2], sign)
    first, second = [], []
    for k in range(count // 2):
        turned = times_const(odd[k], unit(sign * k / count))
        first.append((even[k][0] + turned[0], even[k][1] + turned[1]))
        second.append((even[k][0] - turned[0], even[k][1] - turned[1]))
    return first + second


def lead_forward(values):
    count = len(values)
    twisted = []
    for f, value in enumerate(values):
        w = unit(-f / (4.0 * count))
        twisted.append((value * w.real, value * w.imag))
    return dft(twisted, -1.0)


def lead_inverse(values, scale):
    count = len(values)
    result = []
    for f, (re, im) in enumerate(dft(values, 1.0)):
        w = unit(f / (4.0 * count)) * scale
        result.append(re * w.real - im * w.imag)
    return result


def all_sent(buf, sem, count):
    view = buf.at[pl.ds(0, count - 1)]
    pltpu.make_async_copy(view, view, sem).wait()


def kernel(
    slow_count, fast_count, corr_scale,
    q_ref, k_ref, v_ref, h_ref, o_ref,
    mixed_ref, qgrad_ref, kgrad_ref, vgrad_ref, fgrad_ref,
    send_f, got_f, send_fh, got_fh,
    send_s, got_s, send_sh, got_sh,
    spec, taps, trow, drow, dbuf, mixes,
    send_b, got_b, send_bh, got_bh,
    send_c, got_c, send_ch,
    basis_hi, basis_lo, basis_f32, inv_hi, inv_lo, inv_f32,
    ssem, rsem,
):
    slow = lax.axis_index("slow")
    fast = lax.axis_index("fast")
    S, F = slow_count, fast_count

    barrier = pltpu.get_barrier_semaphore()

    def greet_fast(o, carry):
        pl.semaphore_signal(
            barrier, inc=1, device_id=(slow, lax.rem(fast + o, F)), device_id_type=MESH
        )
        return carry

    def greet_slow(o, carry):
        pl.semaphore_signal(
            barrier, inc=1, device_id=(lax.rem(slow + o, S), fast), device_id_type=MESH
        )
        return carry

    lax.fori_loop(1, F, greet_fast, 0)
    lax.fori_loop(1, S, greet_slow, 0)

    def push(axis, src, dst, which):
        count = F if axis == "fast" else S
        me = fast if axis == "fast" else slow

        def one(o, carry):
            to = lax.rem(me + o, count)
            device = (slow, to) if axis == "fast" else (to, fast)
            pltpu.make_async_remote_copy(
                src_ref=src.at[to],
                dst_ref=dst.at[me],
                send_sem=ssem.at[which],
                recv_sem=rsem.at[which],
                device_id=device,
                device_id_type=MESH,
            ).start()
            return carry

        lax.fori_loop(1, count, one, 0)
        dst[me] = src[me]

    product = (k_ref[...].astype(f32) * v_ref[...].astype(f32)).T
    send_f[:, 0:16, :] = product.reshape(F, 16, LANES).astype(bf16)
    grad_in = (o_ref[...].astype(f32) * q_ref[...].astype(f32)).T
    send_f[:, 16:32, :] = grad_in.reshape(F, 16, LANES).astype(bf16)
    send_fh[...] = h_ref[...]
    pl.semaphore_wait(barrier, F + S - 2)
    push("fast", send_fh, got_fh, 0)
    push("fast", send_f, got_f, 1)

    b = lax.broadcasted_iota(jnp.int32, (LANES, LANES), 0)
    k2 = lax.broadcasted_iota(jnp.int32, (LANES, LANES), 1)
    period = 4 * LANES * F
    phase = jnp.bitwise_and((4 * slow + 1) * b + 4 * F * (k2 * b), period - 1)
    angle = phase.astype(f32) * (2.0 * math.pi / period)
    wr, wi = jnp.cos(angle), -jnp.sin(angle)
    basis_f32[0:LANES, 0:LANES] = wr
    basis_f32[0:LANES, LANES:] = wi
    basis_f32[LANES:, 0:LANES] = -wi
    basis_f32[LANES:, LANES:] = wr
    wrt, wit = wr.T, wi.T
    inv_f32[0:LANES, 0:LANES] = wrt
    inv_f32[0:LANES, LANES:] = -wit
    inv_f32[LANES:, 0:LANES] = wit
    inv_f32[LANES:, LANES:] = wrt
    for full, hi, lo in ((basis_f32, basis_hi, basis_lo), (inv_f32, inv_hi, inv_lo)):
        top = full[...].astype(bf16)
        hi[...] = top
        lo[...] = (full[...] - top.astype(f32)).astype(bf16)

    for at in range(BLOCK - 1):
        spec[at] = jnp.zeros((32, 2 * LANES), f32)
        taps[at] = jnp.zeros((8, 2 * LANES), f32)

    all_sent(got_fh, rsem.at[0], F)
    for k, (re, im) in enumerate(lead_forward([got_fh[f] for f in range(F)])):
        send_sh[k, :, 0:LANES] = re
        send_sh[k, :, LANES:] = im
    push("slow", send_sh, got_sh, 2)
    all_sent(got_f, rsem.at[1], F)

    def lead(g, carry):
        rows = pl.ds(pl.multiple_of(g * 16, 16), 16)
        out = lead_forward([got_f[f, rows, :].astype(f32) for f in range(F)])
        for k, (re, im) in enumerate(out):
            send_s[k, rows, 0:LANES] = re.astype(bf16)
            send_s[k, rows, LANES:] = im.astype(bf16)
        return carry

    lax.fori_loop(0, 2, lead, 0)
    push("slow", send_s, got_s, 3)

    all_sent(got_sh, rsem.at[2], S)
    for i in range(S):
        trow[i : i + 1, :] = got_sh[i]
    tap_spec = jnp.dot(
        trow[0:S, :], basis_f32[...], precision=lax.Precision.HIGHEST, preferred_element_type=f32
    )
    trow[0:8, :] = jnp.zeros((8, 2 * LANES), f32)
    trow[8 : 8 + S, :] = tap_spec
    before = trow[7 : 7 + S, :]
    tap_re = tap_spec[:, 0:LANES] - before[:, LANES:]
    tap_im = tap_spec[:, LANES:] + before[:, 0:LANES]
    for d in range(S):
        taps[BLOCK - 1 + d, :, 0:LANES] = jnp.broadcast_to(tap_re[d : d + 1], (8, LANES))
        taps[BLOCK - 1 + d, :, LANES:] = jnp.broadcast_to(tap_im[d : d + 1], (8, LANES))

    all_sent(got_s, rsem.at[3], S)
    step = min(8, S)

    def to_spec(n, carry):
        at = pl.multiple_of(n * step, step)
        x = got_s[pl.ds(at, step)].reshape(step * 32, 2 * LANES)
        y = jnp.dot(x, basis_hi[...], preferred_element_type=f32)
        y += jnp.dot(x, basis_lo[...], preferred_element_type=f32)
        spec[pl.ds(at + BLOCK - 1, step)] = y.reshape(step, 32, 2 * LANES)
        return carry

    lax.fori_loop(0, S // step, to_spec, 0)

    def part(at, row, im):
        lo = LANES if im else 0
        return spec[at, row : row + 8, lo : lo + LANES]

    zero = jnp.zeros((8, LANES), f32)
    off = BLOCK - 1

    def convolve(J, carry):
        def inner(i, acc):
            rows = [(part(off + i, r, False), part(off + i, r, True)) for r in (0, 8)]
            result = []
            for jj in range(BLOCK):
                d = off + BLOCK * J + jj - i
                hr, hi = taps[d, :, 0:LANES], taps[d, :, LANES:]
                for n, (pr, pi) in enumerate(rows):
                    re, im = acc[2 * jj + n]
                    result.append((re + (hr * pr - hi * pi), im + (hr * pi + hi * pr)))
            return tuple(result)

        acc = lax.fori_loop(0, BLOCK * (J + 1), inner, ((zero, zero),) * (2 * BLOCK))
        for jj in range(BLOCK):
            for n in range(2):
                re, im = acc[2 * jj + n]
                mixes[BLOCK * J + jj, 8 * n : 8 * n + 8, 0:LANES] = re
                mixes[BLOCK * J + jj, 8 * n : 8 * n + 8, LANES:] = im
        return carry

    def correlate(J, carry):
        def inner(i, accs):
            acc, cor = accs
            rows = [(part(off + i, r, False), part(off + i, r, True)) for r in (16, 24)]
            result, sums = [], []
            for jj in range(BLOCK):
                d = off + i - BLOCK * J - jj
                hr, hi = taps[d, :, 0:LANES], taps[d, :, LANES:]
                cr, ci = cor[jj]
                for n, (gr, gi) in enumerate(rows):
                    re, im = acc[2 * jj + n]
                    result.append((re + (hr * gr + hi * gi), im + (hr * gi - hi * gr)))
                    pr, pi = part(d, 8 * n, False), part(d, 8 * n, True)
                    cr = cr + (gr * pr + gi * pi)
                    ci = ci + (gi * pr - gr * pi)
                sums.append((cr, ci))
            return tuple(result), tuple(sums)

        acc, cor = lax.fori_loop(
            BLOCK * J, S, inner, (((zero, zero),) * (2 * BLOCK), ((zero, zero),) * BLOCK)
        )
        for jj in range(BLOCK):
            for n in range(2):
                re, im = acc[2 * jj + n]
                mixes[BLOCK * J + jj, 16 + 8 * n : 24 + 8 * n, 0:LANES] = re
                mixes[BLOCK * J + jj, 16 + 8 * n : 24 + 8 * n, LANES:] = im
            cr, ci = cor[jj]
            dbuf[BLOCK * J + jj, :, 0:LANES] = jnp.sum(cr, axis=0, keepdims=True)
            dbuf[BLOCK * J + jj, :, LANES:] = jnp.sum(ci, axis=0, keepdims=True)
        return carry

    lax.fori_loop(0, S // BLOCK, convolve, 0)
    lax.fori_loop(0, S // BLOCK, correlate, 0)

    def from_spec(n, carry):
        at = pl.ds(pl.multiple_of(n * step, step), step)
        z = mixes[at].reshape(step * 32, 2 * LANES)
        hi = z.astype(bf16)
        lo = (z - hi.astype(f32)).astype(bf16)
        y = jnp.dot(hi, inv_hi[...], preferred_element_type=f32)
        y += jnp.dot(hi, inv_lo[...], preferred_element_type=f32)
        y += jnp.dot(lo, inv_hi[...], preferred_element_type=f32)
        send_b[at] = y.reshape(step, 32, 2 * LANES).astype(bf16)
        return carry

    lax.fori_loop(0, S // step, from_spec, 0)
    push("slow", send_b, got_b, 4)

    drow[...] = jnp.zeros(drow.shape, f32)
    for j in range(S):
        drow[j : j + 1, :] = dbuf[j]
    here, after = drow[0:S, :], drow[1 : S + 1, :]
    corr = jnp.concatenate(
        (here[:, 0:LANES] + after[:, LANES:], here[:, LANES:] - after[:, 0:LANES]), axis=1
    )
    corr = jnp.dot(
        corr, inv_f32[...], precision=lax.Precision.HIGHEST, preferred_element_type=f32
    )
    for j in range(S):
        send_bh[j] = corr[j : j + 1, :]
    push("slow", send_bh, got_bh, 5)

    scale = 1.0 / (LANES * F)
    all_sent(got_b, rsem.at[4], S)

    def unlead(g, carry):
        rows = pl.ds(pl.multiple_of(g * 16, 16), 16)
        values = [
            (got_b[k, rows, 0:LANES].astype(f32), got_b[k, rows, LANES:].astype(f32))
            for k in range(F)
        ]
        for f, out in enumerate(lead_inverse(values, scale)):
            send_c[f, rows, :] = out.astype(bf16)
        return carry

    lax.fori_loop(0, 2, unlead, 0)
    push("fast", send_c, got_c, 6)
    all_sent(got_bh, rsem.at[5], S)
    values = [(got_bh[k, :, 0:LANES], got_bh[k, :, LANES:]) for k in range(F)]
    for f, out in enumerate(lead_inverse(values, scale * corr_scale)):
        send_ch[f] = out
    push("fast", send_ch, fgrad_ref, 7)

    all_sent(got_c, rsem.at[6], F)
    convolved = got_c[:, 0:16, :].astype(f32).reshape(F * 16, LANES).T
    mixed_ref[...] = (q_ref[...].astype(f32) * convolved).astype(bf16)
    qgrad_ref[...] = (o_ref[...].astype(f32) * convolved).astype(bf16)
    backward = got_c[:, 16:32, :].astype(f32).reshape(F * 16, LANES).T
    kgrad_ref[...] = (backward * v_ref[...].astype(f32)).astype(bf16)
    vgrad_ref[...] = (backward * k_ref[...].astype(f32)).astype(bf16)
    all_sent(fgrad_ref, rsem.at[7], F)

    for which, buf, count in (
        (0, send_fh, F), (1, send_f, F), (2, send_sh, S), (3, send_s, S),
        (4, send_b, S), (5, send_bh, S), (6, send_c, F), (7, send_ch, F),
    ):
        all_sent(buf, ssem.at[which], count)


def on_device(slow_count, fast_count, query_act, key_act, value_act, long_filter, out_grad):
    tokens, channels = query_act.shape
    groups = long_filter.shape[1]
    S, F = slow_count, fast_count
    width = channels // groups
    seq_length = tokens * S * F
    corr_scale = 1.0 / math.sqrt(seq_length * width)
    rows = 2 * width
    taps_rows = jnp.transpose(long_filter.astype(f32)).reshape(groups, 1, tokens)
    wide = jax.ShapeDtypeStruct((tokens, channels), bf16)
    vmem = pl.BlockSpec(memory_space=pltpu.VMEM)

    def chunks(count, height, lanes, kind):
        return pltpu.VMEM((count, height, lanes), kind)

    L, L2 = LANES, 2 * LANES
    outs = pl.pallas_call(
        functools.partial(kernel, S, F, corr_scale),
        out_shape=(wide, wide, wide, wide, jax.ShapeDtypeStruct((groups, 1, tokens), f32)),
        in_specs=[vmem] * 5,
        out_specs=(vmem,) * 5,
        scratch_shapes=[
            chunks(F, rows, L, bf16), chunks(F, rows, L, bf16),
            chunks(F, 1, L, f32), chunks(F, 1, L, f32),
            chunks(S, rows, L2, bf16), chunks(S, rows, L2, bf16),
            chunks(S, 1, L2, f32), chunks(S, 1, L2, f32),
            chunks(S + BLOCK - 1, rows, L2, f32),
            chunks(S + BLOCK - 1, 8, L2, f32),
            pltpu.VMEM((S + 8, L2), f32),
            pltpu.VMEM((S + 8, L2), f32),
            chunks(S, 1, L2, f32),
            chunks(S, rows, L2, f32),
            chunks(S, rows, L2, bf16), chunks(S, rows, L2, bf16),
            chunks(S, 1, L2, f32), chunks(S, 1, L2, f32),
            chunks(F, rows, L, bf16), chunks(F, rows, L, bf16),
            chunks(F, 1, L, f32),
            pltpu.VMEM((L2, L2), bf16), pltpu.VMEM((L2, L2), bf16), pltpu.VMEM((L2, L2), f32),
            pltpu.VMEM((L2, L2), bf16), pltpu.VMEM((L2, L2), bf16), pltpu.VMEM((L2, L2), f32),
            pltpu.SemaphoreType.DMA((8,)),
            pltpu.SemaphoreType.DMA((8,)),
        ],
        compiler_params=pltpu.CompilerParams(
            collective_id=0, has_side_effects=True, vmem_limit_bytes=40 << 20
        ),
    )(query_act, key_act, value_act, taps_rows, out_grad)
    filter_grad = jnp.transpose(outs[4].reshape(groups, tokens))
    return outs[0], outs[1], outs[2], outs[3], filter_grad


def solution(mesh):
    placed = P(("slow", "fast"), None)
    return jax.shard_map(
        functools.partial(on_device, mesh.shape["slow"], mesh.shape["fast"]),
        mesh=mesh,
        in_specs=(placed,) * 5,
        out_specs=(placed,) * 5,
        check_vma=False,
    )
```

time: 373 us -> 103 us (0.28); the launches traced: 367 us -> 102 us
  waiting for transfers between devices: 186 us -> 0 us
  Pallas kernels: 0 us -> 93.7 us
  starting transfers between devices: 89.9 us -> 0 us
  blocking collectives: 39 us -> 0 us
  matrix products: 25.5 us -> 0 us
  local copies, waits for them, and re-layouts: 18.5 us -> 6.84 us
  other arithmetic: 5.82 us -> 0.7 us
    all_to_all x12 -> x0, waiting for transfers between devices: 186 us -> none  [the longest x2 41.1 us: spread_forward(): lax.all_to_all(re_im[0], 'fast', split_axis=2, concat_axis=3, tiled=True)]
    pallas_call x0 -> x1, Pallas kernels: none -> 93.7 us  [on_device(): pl.pallas_call(functools.partial(kernel, S, F, corr_scale), out_shape=(wi...]
    all_to_all x12 -> x0, starting transfers between devices: 89.9 us -> none  [the longest x2 20.6 us: spread_inverse(): lax.all_to_all(re_im[1], 'slow', split_axis=2, concat_axis=1, tiled=True)]
    all_to_all x2 -> x0, blocking collectives: 39 us -> none  [the longest x1 24.3 us: spread_inverse(): lax.all_to_all(re_im[0], 'fast', split_axis=3, concat_axis=2, tiled=True)]
    dot_general x48 -> x0, matrix products: 25.5 us -> none  [contract(): jnp.tensordot(values, matrix, axes=((along,), (1,)), precision=highest)]
    add x6 -> x0, local copies, waits for them, and re-layouts: 5.35 us -> none  [the longest x4 3.57 us: apply_dft(): contract(re_im[0], sine_part) + contract(re_im[1], cosine)]
    sub x6 -> x0, local copies, waits for them, and re-layouts: 4.64 us -> none  [the longest x4 2.86 us: apply_dft(): contract(re_im[0], cosine) - contract(re_im[1], sine_part)]
  transfers between devices with their start and end apart: 12 -> 0, of which waited for: 12 -> 0; matrix products, arithmetic and copies ran while one was open for 3% -> 0% of each run, Pallas kernels for 0% -> 0%
where the time goes in v1:
time: 103 us; the launch traced here: 102 us
  Pallas kernels  93.7 us (91%)
  local copies, waits for them, and re-layouts  6.84 us (7%)
    pallas_call x1, Pallas kernels, on_device(): pl.pallas_call(functools.partial(kernel, S, F, corr_scale), out_shape=(wi...  93.7 us
    unnamed x13, local copies, waits for them, and re-layouts  6.84 us

profile of v1, /device:TPU:1, one launch (start us, length us, event | category | flops | bytes accessed | tf_op | source)
XLA Modules:
  0.0 101.9 jit_solution(11008173331231749959)
XLA Ops:
  0.6 0.7 reshape.23
  1.3 0.0 copy-start
  1.3 0.9 copy-done
  2.2 0.0 copy-start.1
  2.2 0.9 copy-done.1
  3.1 0.0 copy-start.2
  3.1 0.9 copy-done.2
  4.0 0.0 copy-start.3
  4.0 0.9 copy-done.3
  5.0 93.7 %shard_map.92 = (bf16[128,512]{1,0:T(8,128)(2,1)S(1)}, bf16[128,512]{1,0:T(8,128)(2,1)S(1)}, bf16[128,512]{1,0:T(8,128)(2,1)S(1)}, bf16[128,512]{1,0:T(8,128)(2,1)S(1)}, f32[32,1,128]{2,1,0:T(1,128)S(1)}) custom-call(bf16[128,512]{1,0:T(8,128)(2,1)S(1)} %copy-done, bf16[128,512]{1,0:T(8,128)(2,1)S(1)} %copy-done.1, bf16[128,512]{1,0:T(8,128)(2,1)S(1)} %copy-done.2, ...), custom_call_target="tpu_custom_call" | custom-call | tf_op jit(solution)/shard_map/pallas_call | solution.py:344
  98.7 0.7 copy.15
  99.3 0.7 copy.16
  100.0 0.7 copy.17
  100.6 0.7 copy.18
  101.3 0.6 copy.19
Async XLA Ops:
  1.3 0.9 copy-start
  2.2 0.9 copy-start.1
  3.1 0.9 copy-start.2
  4.0 0.9 copy-start.3

commit v2 on v1

v2 whole, which is shorter than its diff:
```python
import functools
import math

import jax
import jax.numpy as jnp
from jax import lax
from jax.experimental import pallas as pl
from jax.experimental.pallas import tpu as pltpu
from jax.sharding import PartitionSpec as P

MESH = pl.DeviceIdType.MESH
f32 = jnp.float32
bf16 = jnp.bfloat16
LANES = 128
PARTS = 4
ROWS = 8


def times_const(value, factor):
    re, im = value
    a, b = factor.real, factor.imag
    if abs(b) < 1e-12:
        if abs(a - 1.0) < 1e-12:
            return re, im
        return re * a, im * a
    if abs(a) < 1e-12:
        return (-im, re) if b > 0 else (im, -re)
    return re * a - im * b, re * b + im * a


def unit(turns):
    return complex(math.cos(2.0 * math.pi * turns), math.sin(2.0 * math.pi * turns))


def dft(values, sign):
    count = len(values)
    if count == 1:
        return values
    even, odd = dft(values[0::2], sign), dft(values[1::2], sign)
    first, second = [], []
    for k in range(count // 2):
        turned = times_const(odd[k], unit(sign * k / count))
        first.append((even[k][0] + turned[0], even[k][1] + turned[1]))
        second.append((even[k][0] - turned[0], even[k][1] - turned[1]))
    return first + second


def lead_forward(values):
    count = len(values)
    twisted = []
    for f, value in enumerate(values):
        w = unit(-f / (4.0 * count))
        twisted.append((value * w.real, value * w.imag))
    return dft(twisted, -1.0)


def lead_inverse(values, scale):
    count = len(values)
    result = []
    for f, (re, im) in enumerate(dft(values, 1.0)):
        w = unit(f / (4.0 * count)) * scale
        result.append(re * w.real - im * w.imag)
    return result


def arrived(buf, sem, count):
    view = buf.at[pl.ds(0, count - 1)]
    pltpu.make_async_copy(view, view, sem).wait()


def for_peers(me, ring, side, visit):
    fast_major = side == 2
    at = lax.rem(me, ring) if fast_major else lax.div(me, side)
    beside = lax.div(me, ring) if fast_major else lax.rem(me, side)

    def at_distance(d, skip):
        there = lax.rem(at + d, ring)
        for a in range(skip, side):
            other = lax.rem(beside + a, side)
            visit(other * ring + there if fast_major else there * side + other)

    half = ring // 2
    if half:
        at_distance(half, 0)

    def pair(i, carry):
        at_distance(half - i, 0)
        at_distance(half + i, 0)
        return carry

    if half > 1:
        lax.fori_loop(1, half, pair, 0)
    at_distance(0, 1)


def exchange_kernel(
    S, F, corr_scale,
    q_hbm, k_hbm, v_hbm, h_hbm, o_hbm,
    mixed_out_hbm, corr_hbm,
    q_ref, k_ref, v_ref, h_ref, o_ref,
    send_f, got_f, send_fh, got_fh,
    send_s, got_s, send_sh, got_sh,
    spec, taps, trow, drow, dbuf, mixes,
    send_b, got_b, send_bh, got_bh,
    send_c, send_ch,
    basis_hi, basis_lo, basis_f32, inv_hi, inv_lo, inv_f32,
    ssem, rsem, lsem,
):
    slow = lax.axis_index("slow")
    fast = lax.axis_index("fast")
    block = min(8, S)
    off = block - 1

    loads = [
        pltpu.make_async_copy(src, dst, lsem.at[n])
        for n, (src, dst) in enumerate(
            ((k_hbm, k_ref), (v_hbm, v_ref), (h_hbm, h_ref), (o_hbm, o_ref), (q_hbm, q_ref))
        )
    ]
    barrier = pltpu.get_barrier_semaphore()

    def greet_fast(to):
        pl.semaphore_signal(barrier, inc=1, device_id=(slow, to), device_id_type=MESH)

    def greet_slow(to):
        pl.semaphore_signal(barrier, inc=1, device_id=(to, fast), device_id_type=MESH)

    for_peers(fast, F // 2, 2, greet_fast)
    for_peers(slow, S // 4, 4, greet_slow)
    for load in loads:
        load.start()

    def push(axis, src, dst, which):
        def one(to):
            pltpu.make_async_remote_copy(
                src_ref=src.at[to],
                dst_ref=dst.at[fast if axis == "fast" else slow],
                send_sem=ssem.at[which],
                recv_sem=rsem.at[which],
                device_id=(slow, to) if axis == "fast" else (to, fast),
                device_id_type=MESH,
            ).start()

        if axis == "fast":
            for_peers(fast, F // 2, 2, one)
        else:
            for_peers(slow, S // 4, 4, one)

    for load in loads[:3]:
        load.wait()
    for g, row in enumerate(jnp.split(h_ref[...].astype(f32), F)):
        send_fh[g] = row
    product = (k_ref[...].astype(f32) * v_ref[...].astype(f32)).T.reshape(F, 16, LANES)
    send_f[0] = product[:, 0:8].astype(bf16)
    send_f[2] = product[:, 8:16].astype(bf16)
    pl.semaphore_wait(barrier, F + S - 2)
    push("fast", send_fh, got_fh, 4)
    push("fast", send_f.at[0], got_f.at[0], 0)
    for load in loads[3:]:
        load.wait()
    grad_in = (o_ref[...].astype(f32) * q_ref[...].astype(f32)).T.reshape(F, 16, LANES)
    send_f[1] = grad_in[:, 0:8].astype(bf16)
    send_f[3] = grad_in[:, 8:16].astype(bf16)
    for part in range(1, PARTS):
        push("fast", send_f.at[part], got_f.at[part], part)
    got_fh[fast] = send_fh[fast]
    for part in range(PARTS):
        got_f[part, fast] = send_f[part, fast]

    b = lax.broadcasted_iota(jnp.int32, (LANES, LANES), 0)
    k2 = lax.broadcasted_iota(jnp.int32, (LANES, LANES), 1)
    period = 4 * LANES * F
    phase = jnp.bitwise_and((4 * slow + 1) * b + 4 * F * (k2 * b), period - 1)
    angle = phase.astype(f32) * (2.0 * math.pi / period)
    wr, wi = jnp.cos(angle), -jnp.sin(angle)
    basis_f32[0:LANES, 0:LANES] = wr
    basis_f32[0:LANES, LANES:] = wi
    basis_f32[LANES:, 0:LANES] = -wi
    basis_f32[LANES:, LANES:] = wr
    wrt, wit = wr.T, wi.T
    inv_f32[0:LANES, 0:LANES] = wrt
    inv_f32[0:LANES, LANES:] = -wit
    inv_f32[LANES:, 0:LANES] = wit
    inv_f32[LANES:, LANES:] = wrt
    for full, hi, lo in ((basis_f32, basis_hi, basis_lo), (inv_f32, inv_hi, inv_lo)):
        top = full[...].astype(bf16)
        hi[...] = top
        lo[...] = (full[...] - top.astype(f32)).astype(bf16)

    for at in range(off):
        spec[0, at] = jnp.zeros((ROWS, 2 * LANES), f32)
        spec[2, at] = jnp.zeros((ROWS, 2 * LANES), f32)
        taps[at] = jnp.zeros((ROWS, 2 * LANES), f32)
    dbuf[...] = jnp.zeros(dbuf.shape, f32)

    arrived(got_fh, rsem.at[4], F)
    for k, (re, im) in enumerate(lead_forward([got_fh[f] for f in range(F)])):
        send_sh[k, :, 0:LANES] = re
        send_sh[k, :, LANES:] = im
    push("slow", send_sh, got_sh, 9)
    got_sh[slow] = send_sh[slow]

    def lead(part, carry):
        arrived(got_f.at[part], rsem.at[part], F)
        out = lead_forward([got_f[part, f].astype(f32) for f in range(F)])
        for k, (re, im) in enumerate(out):
            send_s[part, k, :, 0:LANES] = re.astype(bf16)
            send_s[part, k, :, LANES:] = im.astype(bf16)
        push("slow", send_s.at[part], got_s.at[part], 5 + part)
        got_s[part, slow] = send_s[part, slow]
        return carry

    lax.fori_loop(0, PARTS, lead, 0)

    arrived(got_sh, rsem.at[9], S)
    for i in range(S):
        trow[i : i + 1, :] = got_sh[i]
    tap_spec = jnp.dot(
        trow[0:S, :], basis_f32[...], precision=lax.Precision.HIGHEST, preferred_element_type=f32
    )
    trow[0:8, :] = jnp.zeros((8, 2 * LANES), f32)
    trow[8 : 8 + S, :] = tap_spec
    before = trow[7 : 7 + S, :]
    tap_re = tap_spec[:, 0:LANES] - before[:, LANES:]
    tap_im = tap_spec[:, LANES:] + before[:, 0:LANES]
    for d in range(S):
        taps[off + d, :, 0:LANES] = jnp.broadcast_to(tap_re[d : d + 1], (ROWS, LANES))
        taps[off + d, :, LANES:] = jnp.broadcast_to(tap_im[d : d + 1], (ROWS, LANES))

    step = min(16, S)

    def to_spec(part):
        arrived(got_s.at[part], rsem.at[5 + part], S)

        def some(n, carry):
            at = pl.multiple_of(n * step, step)
            x = got_s[part, pl.ds(at, step)].astype(f32).reshape(step * ROWS, 2 * LANES).astype(bf16)
            y = jnp.dot(x, basis_hi[...], preferred_element_type=f32)
            y += jnp.dot(x, basis_lo[...], preferred_element_type=f32)
            spec[part, pl.ds(at + off, step)] = y.reshape(step, ROWS, 2 * LANES)
            return carry

        lax.fori_loop(0, S // step, some, 0)

    def from_spec(part):
        def some(n, carry):
            at = pl.ds(pl.multiple_of(n * step, step), step)
            z = mixes[at].reshape(step * ROWS, 2 * LANES)
            hi = z.astype(bf16)
            lo = (z - hi.astype(f32)).astype(bf16)
            y = jnp.dot(hi, inv_hi[...], preferred_element_type=f32)
            y += jnp.dot(hi, inv_lo[...], preferred_element_type=f32)
            y += jnp.dot(lo, inv_hi[...], preferred_element_type=f32)
            send_b[part, at] = y.reshape(step, ROWS, 2 * LANES).astype(bf16)
            return carry

        lax.fori_loop(0, S // step, some, 0)
        push("slow", send_b.at[part], got_b.at[part], 10 + part)
        got_b[part, slow] = send_b[part, slow]

    def both(ref, *at):
        return ref[(*at, slice(None), slice(0, LANES))], ref[(*at, slice(None), slice(LANES, None))]

    zero = jnp.zeros((ROWS, LANES), f32)

    def convolve(part):
        def group(J, carry):
            def inner(i, acc):
                pr, pi = both(spec, part, off + i)
                result = []
                for jj in range(block):
                    hr, hi = both(taps, off + block * J + jj - i)
                    re, im = acc[jj]
                    result.append((re + (hr * pr - hi * pi), im + (hr * pi + hi * pr)))
                return tuple(result)

            acc = lax.fori_loop(0, block * (J + 1), inner, ((zero, zero),) * block)
            for jj in range(block):
                mixes[block * J + jj, :, 0:LANES], mixes[block * J + jj, :, LANES:] = acc[jj]
            return carry

        lax.fori_loop(0, S // block, group, 0)

    def correlate(part):
        def group(J, carry):
            def inner(i, accs):
                gr, gi = both(spec, part, off + i)
                result = []
                for jj in range(block):
                    d = off + i - block * J - jj
                    hr, hi = both(taps, d)
                    pr, pi = both(spec, part - 1, d)
                    re, im, cr, ci = accs[jj]
                    result.append((
                        re + (hr * gr + hi * gi), im + (hr * gi - hi * gr),
                        cr + (gr * pr + gi * pi), ci + (gi * pr - gr * pi),
                    ))
                return tuple(result)

            accs = lax.fori_loop(block * J, S, inner, ((zero,) * 4,) * block)
            for jj in range(block):
                re, im, cr, ci = accs[jj]
                mixes[block * J + jj, :, 0:LANES] = re
                mixes[block * J + jj, :, LANES:] = im
                dbuf[block * J + jj, :, 0:LANES] += jnp.sum(cr, axis=0, keepdims=True)
                dbuf[block * J + jj, :, LANES:] += jnp.sum(ci, axis=0, keepdims=True)
            return carry

        lax.fori_loop(0, S // block, group, 0)

    def mix(n, carry):
        to_spec(2 * n)
        convolve(2 * n)
        from_spec(2 * n)
        to_spec(2 * n + 1)
        correlate(2 * n + 1)
        from_spec(2 * n + 1)
        return carry

    lax.fori_loop(0, PARTS // 2, mix, 0)

    drow[...] = jnp.zeros(drow.shape, f32)
    for j in range(S):
        drow[j : j + 1, :] = dbuf[j]
    here, after = drow[0:S, :], drow[1 : S + 1, :]
    corr = jnp.concatenate(
        (here[:, 0:LANES] + after[:, LANES:], here[:, LANES:] - after[:, 0:LANES]), axis=1
    )
    corr = jnp.dot(
        corr, inv_f32[...], precision=lax.Precision.HIGHEST, preferred_element_type=f32
    )
    for j in range(S):
        send_bh[j] = corr[j : j + 1, :]
    push("slow", send_bh, got_bh, 14)
    got_bh[slow] = send_bh[slow]

    scale = 1.0 / (LANES * F)

    def unlead(part, carry):
        arrived(got_b.at[part], rsem.at[10 + part], S)
        values = []
        for k in range(F):
            re, im = both(got_b, part, k)
            values.append((re.astype(f32), im.astype(f32)))
        for f, out in enumerate(lead_inverse(values, scale)):
            send_c[part, f] = out.astype(bf16)
        push("fast", send_c.at[part], mixed_out_hbm.at[part], 15 + part)
        pltpu.make_async_copy(
            send_c.at[part, fast], mixed_out_hbm.at[part, fast], lsem.at[5 + part]
        ).start()
        return carry

    lax.fori_loop(0, PARTS, unlead, 0)
    arrived(got_bh, rsem.at[14], S)
    values = [both(got_bh, k) for k in range(F)]
    for f, out in enumerate(lead_inverse(values, scale * corr_scale)):
        send_ch[f] = out
    push("fast", send_ch, corr_hbm, 19)
    own = pltpu.make_async_copy(send_ch.at[fast], corr_hbm.at[fast], lsem.at[9])
    own.start()

    for part in range(PARTS):
        arrived(send_f.at[part], ssem.at[part], F)
        arrived(send_s.at[part], ssem.at[5 + part], S)
        arrived(send_b.at[part], ssem.at[10 + part], S)
        arrived(send_c.at[part], ssem.at[15 + part], F)
        pltpu.make_async_copy(
            send_c.at[part, fast], mixed_out_hbm.at[part, fast], lsem.at[5 + part]
        ).wait()
        arrived(mixed_out_hbm.at[part], rsem.at[15 + part], F)
    for which, buf, count in ((4, send_fh, F), (9, send_sh, S), (14, send_bh, S), (19, send_ch, F)):
        arrived(buf, ssem.at[which], count)
    own.wait()
    arrived(corr_hbm, rsem.at[19], F)


def gate_kernel(
    c_hbm, corr_hbm, q_hbm, k_hbm, v_hbm, o_hbm,
    mixed_hbm, qgrad_hbm, kgrad_hbm, vgrad_hbm, fgrad_hbm,
    c_ref, corr_ref, q_ref, k_ref, v_ref, o_ref,
    mixed_ref, qgrad_ref, kgrad_ref, vgrad_ref, fgrad_ref, sem,
):
    groups, tokens = corr_ref.shape[0], corr_ref.shape[2]
    loads = [
        pltpu.make_async_copy(src, dst, sem.at[n])
        for n, (src, dst) in enumerate((
            (c_hbm, c_ref), (q_hbm, q_ref), (o_hbm, o_ref),
            (k_hbm, k_ref), (v_hbm, v_ref), (corr_hbm, corr_ref),
        ))
    ]
    for load in loads:
        load.start()

    def channels(part):
        low, high = c_ref[part].astype(f32), c_ref[part + 2].astype(f32)
        return jnp.concatenate((low, high), axis=1).reshape(groups * 16, tokens).T

    stores = []

    def store(src, dst):
        stores.append(pltpu.make_async_copy(src, dst, sem.at[len(loads) + len(stores)]))
        stores[-1].start()

    for load in loads[:3]:
        load.wait()
    convolved = channels(0)
    mixed_ref[...] = (q_ref[...].astype(f32) * convolved).astype(bf16)
    store(mixed_ref, mixed_hbm)
    qgrad_ref[...] = (o_ref[...].astype(f32) * convolved).astype(bf16)
    store(qgrad_ref, qgrad_hbm)
    for load in loads[3:]:
        load.wait()
    backward = channels(1)
    kgrad_ref[...] = (backward * v_ref[...].astype(f32)).astype(bf16)
    store(kgrad_ref, kgrad_hbm)
    vgrad_ref[...] = (backward * k_ref[...].astype(f32)).astype(bf16)
    store(vgrad_ref, vgrad_hbm)
    fgrad_ref[...] = corr_ref[...].reshape(groups, tokens)
    store(fgrad_ref, fgrad_hbm)
    for done in stores:
        done.wait()


def on_device(S, F, query_act, key_act, value_act, long_filter, out_grad):
    tokens, channels = query_act.shape
    groups = long_filter.shape[1]
    seq_length = tokens * S * F
    corr_scale = 1.0 / math.sqrt(seq_length * (channels // groups))
    wide = jax.ShapeDtypeStruct((tokens, channels), bf16)
    hbm = pl.BlockSpec(memory_space=pltpu.HBM)
    L, L2 = LANES, 2 * LANES
    off = min(8, S) - 1
    wides = [pltpu.VMEM(wide.shape, bf16)] * 4
    parts = jax.ShapeDtypeStruct((PARTS, F, ROWS, tokens), bf16)
    corrs = jax.ShapeDtypeStruct((F, 1, tokens), f32)
    mixed, corr = pl.pallas_call(
        functools.partial(exchange_kernel, S, F, corr_scale),
        out_shape=(parts, corrs),
        in_specs=[hbm] * 5,
        out_specs=(hbm,) * 2,
        scratch_shapes=[
            *wides[:3], pltpu.VMEM((groups, tokens), bf16), wides[3],
            pltpu.VMEM((PARTS, F, ROWS, L), bf16), pltpu.VMEM((PARTS, F, ROWS, L), bf16),
            pltpu.VMEM((F, 1, L), f32), pltpu.VMEM((F, 1, L), f32),
            pltpu.VMEM((PARTS, S, ROWS, L2), bf16), pltpu.VMEM((PARTS, S, ROWS, L2), bf16),
            pltpu.VMEM((S, 1, L2), f32), pltpu.VMEM((S, 1, L2), f32),
            pltpu.VMEM((PARTS, S + off, ROWS, L2), f32),
            pltpu.VMEM((S + off, ROWS, L2), f32),
            pltpu.VMEM((S + 8, L2), f32),
            pltpu.VMEM((S + 8, L2), f32),
            pltpu.VMEM((S, 1, L2), f32),
            pltpu.VMEM((S, ROWS, L2), f32),
            pltpu.VMEM((PARTS, S, ROWS, L2), bf16), pltpu.VMEM((PARTS, S, ROWS, L2), bf16),
            pltpu.VMEM((S, 1, L2), f32), pltpu.VMEM((S, 1, L2), f32),
            pltpu.VMEM((PARTS, F, ROWS, L), bf16),
            pltpu.VMEM((F, 1, L), f32),
            pltpu.VMEM((L2, L2), bf16), pltpu.VMEM((L2, L2), bf16), pltpu.VMEM((L2, L2), f32),
            pltpu.VMEM((L2, L2), bf16), pltpu.VMEM((L2, L2), bf16), pltpu.VMEM((L2, L2), f32),
            pltpu.SemaphoreType.DMA((5 * PARTS,)),
            pltpu.SemaphoreType.DMA((5 * PARTS,)),
            pltpu.SemaphoreType.DMA((10,)),
        ],
        compiler_params=pltpu.CompilerParams(
            collective_id=0, has_side_effects=True, vmem_limit_bytes=63 << 20
        ),
    )(query_act, key_act, value_act, long_filter.T, out_grad)
    fgrad = jax.ShapeDtypeStruct((groups, tokens), f32)
    outs = pl.pallas_call(
        gate_kernel,
        out_shape=(wide, wide, wide, wide, fgrad),
        in_specs=[hbm] * 6,
        out_specs=(hbm,) * 5,
        scratch_shapes=[
            pltpu.VMEM(parts.shape, bf16), pltpu.VMEM(corrs.shape, f32),
            *wides, *wides, pltpu.VMEM(fgrad.shape, f32),
            pltpu.SemaphoreType.DMA((11,)),
        ],
        compiler_params=pltpu.CompilerParams(vmem_limit_bytes=63 << 20),
    )(mixed, corr, query_act, key_act, value_act, out_grad)
    return (*outs[:4], outs[4].T)


def solution(mesh):
    placed = P(("slow", "fast"), None)
    return jax.shard_map(
        functools.partial(on_device, mesh.shape["slow"], mesh.shape["fast"]),
        mesh=mesh,
        in_specs=(placed,) * 5,
        out_specs=(placed,) * 5,
        check_vma=False,
    )
```

time: 103 us -> 73.4 us (0.71)
  Pallas kernels: 93.7 us -> 72.6 us
  local copies, waits for them, and re-layouts: 6.84 us -> 0 us
    pallas_call x1 -> x2, Pallas kernels: 93.7 us -> 72.6 us  [the longest x1 70.5 us: on_device(): pl.pallas_call(functools.partial(exchange_kernel, S, F, corr_scale), out_...]
    unnamed x13 -> x0, local copies, waits for them, and re-layouts: 6.84 us -> none
where the time goes in v2:
time: 73.4 us; the launch traced here: 73.2 us
  Pallas kernels  72.6 us (99%)
    pallas_call x1, Pallas kernels, on_device(): pl.pallas_call(functools.partial(exchange_kernel, S, F, corr_scale), out_...  70.5 us
    pallas_call x1, Pallas kernels, on_device(): pl.pallas_call(gate_kernel, out_shape=(wide, wide, wide, wide, fgrad), in...  2.07 us

profile of v2, /device:TPU:1, one launch (start us, length us, event | category | flops | bytes accessed | tf_op | source)
XLA Modules:
  0.0 73.2 jit_solution(4156465000060337534)
XLA Ops:
  0.6 70.5 %shard_map.92 = (bf16[4,32,8,128]{3,2,1,0:T(8,128)(2,1)}, f32[32,1,128]{2,1,0:T(1,128)}) custom-call(bf16[128,512]{1,0:T(8,128)(2,1)} %q_hbm.3, bf16[128,512]{1,0:T(8,128)(2,1)} %k_hbm.3, bf16[128,512]{1,0:T(8,128)(2,1)} %v_hbm.3, bf16[32,128]{1,0:T(8,128)(2,1)} %bitcast.2, bf16[128,512]{1,0:T(8,128)(2,1)} %o_hbm.3), custom_call_target="tpu_custom_call" | custom-call | tf_op jit(solution)/shard_map/pallas_call | solution.py:436
  71.2 2.1 %shard_map.93 = (bf16[128,512]{1,0:T(8,128)(2,1)}, bf16[128,512]{1,0:T(8,128)(2,1)}, bf16[128,512]{1,0:T(8,128)(2,1)}, bf16[128,512]{1,0:T(8,128)(2,1)}, f32[32,128]{1,0:T(8,128)}) custom-call(bf16[4,32,8,128]{3,2,1,0:T(8,128)(2,1)} %get-tuple-element.12.c_hbm, f32[32,1,128]{2,1,0:T(1,128)} %get-tuple-element.13.corr_hbm, bf16[128,512]{1,0:T(8,128)(2,1)} %q_hbm.3, ...), custom_call_target="tpu_custom_call" | custom-call | tf_op jit(solution)/shard_map/pallas_call | solution.py:468

commit v3 on v2

--- a/solution.py
+++ b/solution.py
@@ -210,7 +210,7 @@
         got_s[part, slow] = send_s[part, slow]
         return carry
 
-    lax.fori_loop(0, PARTS, lead, 0)
+    lax.fori_loop(0, PARTS - 1, lead, 0)
 
     arrived(got_sh, rsem.at[9], S)
     for i in range(S):
@@ -227,6 +227,8 @@
         taps[off + d, :, 0:LANES] = jnp.broadcast_to(tap_re[d : d + 1], (ROWS, LANES))
         taps[off + d, :, LANES:] = jnp.broadcast_to(tap_im[d : d + 1], (ROWS, LANES))
 
+    lead(PARTS - 1, 0)
+
     step = min(16, S)
 
     def to_spec(part):
@@ -281,43 +283,71 @@
 
         lax.fori_loop(0, S // block, group, 0)
 
-    def correlate(part):
+    def adjoint(part):
         def group(J, carry):
-            def inner(i, accs):
+            def inner(i, acc):
                 gr, gi = both(spec, part, off + i)
                 result = []
                 for jj in range(block):
-                    d = off + i - block * J - jj
-                    hr, hi = both(taps, d)
-                    pr, pi = both(spec, part - 1, d)
-                    re, im, cr, ci = accs[jj]
-                    result.append((
-                        re + (hr * gr + hi * gi), im + (hr * gi - hi * gr),
-                        cr + (gr * pr + gi * pi), ci + (gi * pr - gr * pi),
-                    ))
+                    hr, hi = both(taps, off + i - block * J - jj)
+                    re, im = acc[jj]
+                    result.append((re + (hr * gr + hi * gi), im + (hr * gi - hi * gr)))
                 return tuple(result)
 
-            accs = lax.fori_loop(block * J, S, inner, ((zero,) * 4,) * block)
+            acc = lax.fori_loop(block * J, S, inner, ((zero, zero),) * block)
             for jj in range(block):
-                re, im, cr, ci = accs[jj]
-                mixes[block * J + jj, :, 0:LANES] = re
-                mixes[block * J + jj, :, LANES:] = im
-                dbuf[block * J + jj, :, 0:LANES] += jnp.sum(cr, axis=0, keepdims=True)
-                dbuf[block * J + jj, :, LANES:] += jnp.sum(ci, axis=0, keepdims=True)
+                mixes[block * J + jj, :, 0:LANES], mixes[block * J + jj, :, LANES:] = acc[jj]
             return carry
 
         lax.fori_loop(0, S // block, group, 0)
 
-    def mix(n, carry):
-        to_spec(2 * n)
-        convolve(2 * n)
-        from_spec(2 * n)
-        to_spec(2 * n + 1)
-        correlate(2 * n + 1)
-        from_spec(2 * n + 1)
+    def correlate(part):
+        def group(J, carry):
+            def inner(i, acc):
+                gr, gi = both(spec, part, off + i)
+                result = []
+                for jj in range(block):
+                    pr, pi = both(spec, part - 1, off + i - block * J - jj)
+                    re, im = acc[jj]
+                    result.append((re + (gr * pr + gi * pi), im + (gi * pr - gr * pi)))
+                return tuple(result)
+
+            acc = lax.fori_loop(block * J, S, inner, ((zero, zero),) * block)
+            for jj in range(block):
+                re, im = acc[jj]
+                dbuf[block * J + jj, :, 0:LANES] += jnp.sum(re, axis=0, keepdims=True)
+                dbuf[block * J + jj, :, LANES:] += jnp.sum(im, axis=0, keepdims=True)
+            return carry
+
+        lax.fori_loop(0, S // block, group, 0)
+
+    scale = 1.0 / (LANES * F)
+
+    def unlead(part, carry):
+        arrived(got_b.at[part], rsem.at[10 + part], S)
+        values = []
+        for k in range(F):
+            re, im = both(got_b, part, k)
+            values.append((re.astype(f32), im.astype(f32)))
+        for f, out in enumerate(lead_inverse(values, scale)):
+            send_c[part, f] = out.astype(bf16)
+        push("fast", send_c.at[part], mixed_out_hbm.at[part], 15 + part)
+        pltpu.make_async_copy(
+            send_c.at[part, fast], mixed_out_hbm.at[part, fast], lsem.at[5 + part]
+        ).start()
         return carry
 
-    lax.fori_loop(0, PARTS // 2, mix, 0)
+    for part in range(PARTS):
+        to_spec(part)
+        if part % 2:
+            adjoint(part)
+        else:
+            convolve(part)
+        from_spec(part)
+        if part == 1:
+            correlate(part)
+    unlead(0, 0)
+    correlate(PARTS - 1)
 
     drow[...] = jnp.zeros(drow.shape, f32)
     for j in range(S):
@@ -334,23 +364,7 @@
     push("slow", send_bh, got_bh, 14)
     got_bh[slow] = send_bh[slow]
 
-    scale = 1.0 / (LANES * F)
-
-    def unlead(part, carry):
-        arrived(got_b.at[part], rsem.at[10 + part], S)
-        values = []
-        for k in range(F):
-            re, im = both(got_b, part, k)
-            values.append((re.astype(f32), im.astype(f32)))
-        for f, out in enumerate(lead_inverse(values, scale)):
-            send_c[part, f] = out.astype(bf16)
-        push("fast", send_c.at[part], mixed_out_hbm.at[part], 15 + part)
-        pltpu.make_async_copy(
-            send_c.at[part, fast], mixed_out_hbm.at[part, fast], lsem.at[5 + part]
-        ).start()
-        return carry
-
-    lax.fori_loop(0, PARTS, unlead, 0)
+    lax.fori_loop(1, PARTS, unlead, 0)
     arrived(got_bh, rsem.at[14], S)
     values = [both(got_bh, k) for k in range(F)]
     for f, out in enumerate(lead_inverse(values, scale * corr_scale)):

time: 73.4 us -> 72.1 us (0.982)
  Pallas kernels: 72.6 us -> 71.3 us
    pallas_call x1, Pallas kernels: 70.5 us -> 69.2 us  [on_device(): pl.pallas_call(functools.partial(exchange_kernel, S, F, corr_scale), out_...]
where the time goes in v3:
time: 72.1 us; the launch traced here: 71.9 us
  Pallas kernels  71.3 us (99%)
    pallas_call x1, Pallas kernels, on_device(): pl.pallas_call(functools.partial(exchange_kernel, S, F, corr_scale), out_...  69.2 us
    pallas_call x1, Pallas kernels, on_device(): pl.pallas_call(gate_kernel, out_shape=(wide, wide, wide, wide, fgrad), in...  2.07 us

profile of v3, /device:TPU:1, one launch (start us, length us, event | category | flops | bytes accessed | tf_op | source)
XLA Modules:
  0.0 71.9 jit_solution(13658175641720290894)
XLA Ops:
  0.6 69.2 %shard_map.92 = (bf16[4,32,8,128]{3,2,1,0:T(8,128)(2,1)}, f32[32,1,128]{2,1,0:T(1,128)}) custom-call(bf16[128,512]{1,0:T(8,128)(2,1)} %q_hbm.3, bf16[128,512]{1,0:T(8,128)(2,1)} %k_hbm.3, bf16[128,512]{1,0:T(8,128)(2,1)} %v_hbm.3, bf16[32,128]{1,0:T(8,128)(2,1)} %bitcast.2, bf16[128,512]{1,0:T(8,128)(2,1)} %o_hbm.3), custom_call_target="tpu_custom_call" | custom-call | tf_op jit(solution)/shard_map/pallas_call | solution.py:450
  69.8 2.1 %shard_map.93 = (bf16[128,512]{1,0:T(8,128)(2,1)}, bf16[128,512]{1,0:T(8,128)(2,1)}, bf16[128,512]{1,0:T(8,128)(2,1)}, bf16[128,512]{1,0:T(8,128)(2,1)}, f32[32,128]{1,0:T(8,128)}) custom-call(bf16[4,32,8,128]{3,2,1,0:T(8,128)(2,1)} %get-tuple-element.12.c_hbm, f32[32,1,128]{2,1,0:T(1,128)} %get-tuple-element.13.corr_hbm, bf16[128,512]{1,0:T(8,128)(2,1)} %q_hbm.3, ...), custom_call_target="tpu_custom_call" | custom-call | tf_op jit(solution)/shard_map/pallas_call | solution.py:482
